TPU v7x, 256 devices: a whole 4x4x8 slice. The times are simulated.
256 devices in a mesh: px: 16 (over z, core), py: 16 (over x, y).
Axes of the slice: x: 4, y: 4, z: 8, core: 2. Of those that a mesh axis runs over, the one named last changes fastest.
Arguments:
- right_side: float32 [64, 128, 1024], P('px', 'py'), may hold values from -40 to 40
- diagonal: float32 [64, 128, 1024], P('px', 'py'), may hold values from 0.05 to 3
- aggregate_id: int32 [64, 128, 1024], P('px', 'py'), may hold values from 0 to 511, as said below
- coarse_diag: float32 [32, 32, 128], P('px', 'py'), may hold values from 150 to 230
- coarse_link: float32 [3, 32, 32, 128], P(None, 'px', 'py'), may hold values from 0.75 to 1.25
Outputs:
- solution_field: float32 [64, 128, 1024], P('px', 'py')
- residual: float32 [64, 128, 1024], P('px', 'py')
Inputs may be any that keep to these rules, and one draw needn't show every extreme that they name: `aggregate_id`: the cell (x, y, z) names the aggregate ((x % 4) // 2) * 2 * 128 + ((y % 8) // 4) * 128 + k of its own partition, where k differs from z // 8 by at most one; every aggregate of every partition holds cells.
All inputs are finite; a program needn't handle non-finite values.
Results may differ from a plain program's by a relative error of at most 0.0003.
Values sent between devices are 32-bit elements; how exact they have to be, the bound alone decides.
No kernel may reach another device: no remote copies, remote signals or barrier semaphores. Data moves between devices by JAX's collectives and lax.ppermute only.
A program may use at most 64 MiB of HBM per device.

v0:
```python
import jax
import jax.numpy as jnp
from jax import lax
from jax.sharding import Mesh
from jax.sharding import PartitionSpec as P

ITERS = 4
PX_PY = ("px_0", "px_1", "py_0", "py_1")
PX = ("px_0", "px_1")
PY = ("py_0", "py_1")
OMEGA = 2.0 / 3.0
FACES = (32.0, 16.0, 8.0)


def padded_2(value, sides, width):
    edges = {}
    for axis, dim in sides:
        peers, length = (lax.axis_size(axis), value.shape[dim])
        up = [(i, (i + 1) % peers) for i in range(peers - 1)]
        last = lax.slice_in_dim(value, length - width, length, axis=dim)
        first = lax.slice_in_dim(value, 0, width, axis=dim)
        edges[dim] = (
            lax.ppermute(last, axis, up),
            lax.ppermute(first, axis, [(b, a) for a, b in up]),
        )
    done = []
    for _, dim in sides:
        low, high = edges[dim]
        around = [(width, width) if d in done else (0, 0) for d in range(value.ndim)]
        value = jnp.concatenate([jnp.pad(low, around), value, jnp.pad(high, around)], axis=dim)
        done.append(dim)
    return value


def with_halo(cells, sides, width):
    for axis, dim in sides:
        count = lax.axis_size(axis)
        ends = count - 1
        head = lax.slice_in_dim(cells, 0, width, axis=dim)
        tail = lax.slice_in_dim(cells, cells.shape[dim] - width, cells.shape[dim], axis=dim)
        cells = jnp.concatenate(
            [
                lax.ppermute(tail, axis, [(i, (i + 1) % count) for i in range(ends)]),
                cells,
                lax.ppermute(head, axis, [((i + 1) % count, i) for i in range(ends)]),
            ],
            axis=dim,
        )
    return cells


def by_axis(value, axes):
    for axis in axes:
        value = lax.psum(value, axis)
    return value


def beside_sum(padded):
    padded = jnp.pad(padded, ((0, 0), (0, 0), (1, 1)))
    beside = padded[2:, 1:-1, 1:-1] + padded[:-2, 1:-1, 1:-1]
    beside = beside + padded[1:-1, 2:, 1:-1] + padded[1:-1, :-2, 1:-1]
    beside = beside + padded[1:-1, 1:-1, 2:] + padded[1:-1, 1:-1, :-2]
    return beside


def apply_fine(values, diagonal):
    widened = padded_2(values, ((PX, 0), (PY, 1)), 1)
    return (6.0 + diagonal) * values - beside_sum(widened)


def coarse_apply(coarse, coarse_diag, weights):
    weighted = weights * coarse[None]
    stacked = jnp.stack((coarse, weighted[0], weighted[1]), axis=0)
    widened = padded_2(stacked, ((PX, 1), (PY, 2)), 1)
    near = weights[0] * widened[0, 2:, 1:-1] + widened[1, :-2, 1:-1]
    near = near + weights[1] * widened[0, 1:-1, 2:] + widened[2, 1:-1, :-2]
    deep_c = jnp.pad(coarse, ((0, 0), (0, 0), (1, 1)))
    deep_w = jnp.pad(weighted[2], ((0, 0), (0, 0), (1, 1)))
    near = near + weights[2] * deep_c[:, :, 2:] + deep_w[:, :, :-2]
    return coarse_diag * coarse - near


def coarse_solve(coarse_rhs, coarse_diag, weights):
    estimate = coarse_rhs / coarse_diag
    for sweep_index in range(2):
        estimate = (
            estimate + (coarse_rhs - coarse_apply(estimate, coarse_diag, weights)) / coarse_diag
        )
    return estimate


def local(right_side, diagonal, aggregate_id, coarse_diag, coarse_link):
    rows_here = right_side.shape[0]
    cols_here = right_side.shape[1]
    depth_here = right_side.shape[2]
    rows_agg = coarse_diag.shape[0]
    cols_agg = coarse_diag.shape[1]
    depth_agg = coarse_diag.shape[2]
    scaling = 6.0 + diagonal
    faces = jnp.array(FACES, dtype=jnp.float32)
    weights = coarse_link * faces[:, None, None, None]
    home = lax.iota(jnp.int32, depth_here) // 8
    offset = aggregate_id % depth_agg - home[None, None, :]
    go_up = offset == 1
    go_down = offset == -1

    def box_sum(values):
        return values.reshape(rows_agg, 2, cols_agg, 4, depth_agg, 8).sum(axis=(1, 3, 5))

    def expand(coarse):
        wide = jnp.broadcast_to(
            coarse[:, None, :, None, :, None], (rows_agg, 2, cols_agg, 4, depth_agg, 8)
        )
        return wide.reshape(rows_here, cols_here, depth_here)

    def restrict(values):
        middle = box_sum(jnp.where(offset == 0, values, 0.0))
        upper = box_sum(jnp.where(go_up, values, 0.0))
        lower = box_sum(jnp.where(go_down, values, 0.0))
        middle = middle + jnp.pad(upper[:, :, :-1], ((0, 0), (0, 0), (1, 0)))
        return middle + jnp.pad(lower[:, :, 1:], ((0, 0), (0, 0), (0, 1)))

    def lift(coarse):
        above = jnp.pad(coarse[:, :, 1:], ((0, 0), (0, 0), (0, 1)))
        below = jnp.pad(coarse[:, :, :-1], ((0, 0), (0, 0), (1, 0)))
        return jnp.where(go_up, expand(above), jnp.where(go_down, expand(below), expand(coarse)))

    diag_wide = with_halo(diagonal, ((PX, 0), (PY, 1)), 2)
    scale_wide = 6.0 + diag_wide
    scale_mid = scale_wide[1:-1, 1:-1]
    row_global = lax.axis_index(PX) * rows_here + lax.iota(jnp.int32, rows_here + 2) - 1
    col_global = lax.axis_index(PY) * cols_here + lax.iota(jnp.int32, cols_here + 2) - 1
    row_inside = (row_global >= 0) & (row_global < rows_here * lax.axis_size(PX))
    col_inside = (col_global >= 0) & (col_global < cols_here * lax.axis_size(PY))
    inside = row_inside[:, None, None] & col_inside[None, :, None]

    def smooth_restrict(vector):
        widened = with_halo(vector, ((PX, 0), (PY, 1)), 2)
        smoothed_wide = OMEGA * widened / scale_wide
        middle = widened[1:-1, 1:-1] - (
            scale_mid * smoothed_wide[1:-1, 1:-1] - beside_sum(smoothed_wide)
        )
        middle = jnp.where(inside, middle, 0.0)
        shrunk = middle / scale_mid
        smoothed = smoothed_wide[2:-2, 2:-2]
        remainder = middle[1:-1, 1:-1]
        reduced = remainder - OMEGA * ((6.0 + diagonal) * shrunk[1:-1, 1:-1] - beside_sum(shrunk))
        return (smoothed, remainder, reduced)

    def precondition(vector):
        smoothed, remainder, reduced = smooth_restrict(vector)
        coarse_rhs = restrict(reduced)
        correction = coarse_solve(coarse_rhs, coarse_diag, weights)
        lifted = lift(correction)
        spread = lifted - OMEGA * apply_fine(lifted, diagonal) / scaling
        leftover = remainder - apply_fine(spread, diagonal)
        return smoothed + spread + OMEGA * leftover / scaling

    solution = jnp.zeros_like(right_side)
    residual = right_side
    shaped = precondition(residual)
    operated = apply_fine(shaped, diagonal)
    for iteration in range(ITERS):
        gamma_now, delta_now = (
            by_axis(jnp.sum(residual * shaped), PX_PY),
            by_axis(jnp.sum(operated * shaped), PX_PY),
        )
        further = iteration + 1 < ITERS
        if further:
            shaped_next = precondition(operated)
            applied_next = apply_fine(shaped_next, diagonal)
        if iteration == 0:
            alpha_now = gamma_now / delta_now
            direction = shaped
            along_dir = operated
            search_pre = shaped_next
            search_img = applied_next
        else:
            beta_now = gamma_now / gamma_old
            alpha_now = gamma_now / (delta_now - beta_now * gamma_now / alpha_old)
            direction = shaped + beta_now * direction
            along_dir = operated + beta_now * along_dir
            if further:
                search_pre = shaped_next + beta_now * search_pre
                search_img = applied_next + beta_now * search_img
        solution = solution + alpha_now * direction
        residual = residual - alpha_now * along_dir
        if further:
            shaped = shaped - alpha_now * search_pre
            operated = operated - alpha_now * search_img
        gamma_old = gamma_now
        alpha_old = alpha_now
    return (solution, residual)


def solution(mesh):
    finer = Mesh(mesh.devices.reshape(8, 2, 4, 4), ("px_0", "px_1", "py_0", "py_1"))
    in_specs = (
        P(PX, PY, None),
        P(PX, PY, None),
        P(PX, PY, None),
        P(PX, PY, None),
        P(None, PX, PY, None),
    )
    out_specs = (P(PX, PY, None), P(PX, PY, None))
    return jax.shard_map(local, mesh=finer, in_specs=in_specs, out_specs=out_specs, check_vma=False)
```

profile of v0, /device:TPU:8, one launch (start us, length us, event | category | flops | bytes accessed | tf_op | source)
XLA Modules:
  0.0 671.6 jit_solution(10432730826388933379)
XLA Ops:
  53.3 5.5 collective-permute-done.8
  60.8 6.0 collective-permute-start.15
  87.1 6.0 collective-permute-start.19
  95.1 5.8 collective-permute-done.18
  116.0 4.3 collective-permute-start.25
  132.4 4.3 collective-permute-start.28
  138.5 5.6 collective-permute-done.29
  175.7 4.6 collective-permute-done.32
  203.2 4.6 collective-permute-start.41
  209.1 6.0 collective-permute-start.43
  217.1 5.5 collective-permute-done.42
  223.1 4.4 collective-permute-start.45
  240.1 5.9 collective-permute-start.49
  253.2 26.3 %all-reduce.95 = (f32[]{:T(128)}, f32[]{:T(128)}) all-reduce(f32[]{:T(128)} %get-tuple-element.9, f32[]{:T(128)} %get-tuple-element.8), channel_id=1, replica_groups=mesh['px_0'=8,'px_1'=2,'py_0'=4,'py_1'=4] {'px_0'}, use_global_device_ids=true, to_apply=%region_4.5 | all-reduce | flops 2 | bytes 16 | tf_op jit(solution)/shard_map/psum | solution.py:54
  282.6 9.8 %all-reduce.103 = (f32[]{:T(128)}, f32[]{:T(128)}) all-reduce(f32[]{:T(128)} %get-tuple-element.40, f32[]{:T(128)} %get-tuple-element.41), channel_id=1, replica_groups=mesh['px_0'=8,'px_1'=2,'py_0'=4,'py_1'=4] {'py_0'}, use_global_device_ids=true, to_apply=%region_6.7 | all-reduce | flops 2 | bytes 16 | tf_op jit(solution)/shard_map/psum | solution.py:54
  292.4 12.4 %all-reduce.99 = (f32[]{:T(128)}, f32[]{:T(128)}) all-reduce(f32[]{:T(128)} %get-tuple-element.32, f32[]{:T(128)} %get-tuple-element.33), channel_id=1, replica_groups=mesh['px_0'=8,'px_1'=2,'py_0'=4,'py_1'=4] {'py_1'}, use_global_device_ids=true, to_apply=%region_7.8 | all-reduce | flops 2 | bytes 16 | tf_op jit(solution)/shard_map/psum | solution.py:54
  316.7 4.1 collective-permute-start.55
  376.7 6.0 collective-permute-start.67
  384.7 5.8 collective-permute-done.66
  416.5 25.0 %all-reduce.94 = (f32[]{:T(128)}, f32[]{:T(128)}) all-reduce(f32[]{:T(128)} %get-tuple-element.7, f32[]{:T(128)} %get-tuple-element.6), channel_id=1, replica_groups=mesh['px_0'=8,'px_1'=2,'py_0'=4,'py_1'=4] {'px_0'}, use_global_device_ids=true, to_apply=%region_17.18 | all-reduce | flops 2 | bytes 16 | tf_op jit(solution)/shard_map/psum | solution.py:54
  444.6 8.6 %all-reduce.102 = (f32[]{:T(128)}, f32[]{:T(128)}) all-reduce(f32[]{:T(128)} %get-tuple-element.38, f32[]{:T(128)} %get-tuple-element.39), channel_id=1, replica_groups=mesh['px_0'=8,'px_1'=2,'py_0'=4,'py_1'=4] {'py_0'}, use_global_device_ids=true, to_apply=%region_19.20 | all-reduce | flops 2 | bytes 16 | tf_op jit(solution)/shard_map/psum | solution.py:54
  453.3 12.3 %all-reduce.98 = (f32[]{:T(128)}, f32[]{:T(128)}) all-reduce(f32[]{:T(128)} %get-tuple-element.30, f32[]{:T(128)} %get-tuple-element.31), channel_id=1, replica_groups=mesh['px_0'=8,'px_1'=2,'py_0'=4,'py_1'=4] {'py_1'}, use_global_device_ids=true, to_apply=%region_20.21 | all-reduce | flops 2 | bytes 16 | tf_op jit(solution)/shard_map/psum | solution.py:54
  480.6 4.1 collective-permute-start.79
  510.4 4.6 collective-permute-start.87
  532.3 6.0 collective-permute-start.91
  540.3 5.8 collective-permute-done.90
  572.1 25.0 %all-reduce.93 = (f32[]{:T(128)}, f32[]{:T(128)}) all-reduce(f32[]{:T(128)} %get-tuple-element.5, f32[]{:T(128)} %get-tuple-element.4), channel_id=1, replica_groups=mesh['px_0'=8,'px_1'=2,'py_0'=4,'py_1'=4] {'px_0'}, use_global_device_ids=true, to_apply=%region_30.31 | all-reduce | flops 2 | bytes 16 | tf_op jit(solution)/shard_map/psum | solution.py:54
  600.2 8.3 %all-reduce.101 = (f32[]{:T(128)}, f32[]{:T(128)}) all-reduce(f32[]{:T(128)} %get-tuple-element.36, f32[]{:T(128)} %get-tuple-element.37), channel_id=1, replica_groups=mesh['px_0'=8,'px_1'=2,'py_0'=4,'py_1'=4] {'py_0'}, use_global_device_ids=true, to_apply=%region_32.33 | all-reduce | flops 2 | bytes 16 | tf_op jit(solution)/shard_map/psum | solution.py:54
  608.5 12.6 %all-reduce.97 = (f32[]{:T(128)}, f32[]{:T(128)}) all-reduce(f32[]{:T(128)} %get-tuple-element.28, f32[]{:T(128)} %get-tuple-element.29), channel_id=1, replica_groups=mesh['px_0'=8,'px_1'=2,'py_0'=4,'py_1'=4] {'py_1'}, use_global_device_ids=true, to_apply=%region_33.34 | all-reduce | flops 2 | bytes 16 | tf_op jit(solution)/shard_map/psum | solution.py:54
  626.2 18.0 %all-reduce.92 = (f32[]{:T(128)}, f32[]{:T(128)}) all-reduce(f32[]{:T(128)} %get-tuple-element.3, f32[]{:T(128)} %get-tuple-element.2), channel_id=1, replica_groups=mesh['px_0'=8,'px_1'=2,'py_0'=4,'py_1'=4] {'px_0'}, use_global_device_ids=true, to_apply=%region_43.44 | all-reduce | flops 2 | bytes 16 | tf_op jit(solution)/shard_map/psum | solution.py:54
  647.3 8.3 %all-reduce.100 = (f32[]{:T(128)}, f32[]{:T(128)}) all-reduce(f32[]{:T(128)} %get-tuple-element.34, f32[]{:T(128)} %get-tuple-element.35), channel_id=1, replica_groups=mesh['px_0'=8,'px_1'=2,'py_0'=4,'py_1'=4] {'py_0'}, use_global_device_ids=true, to_apply=%region_45.46 | all-reduce | flops 2 | bytes 16 | tf_op jit(solution)/shard_map/psum | solution.py:54
  655.7 10.9 %all-reduce.96 = (f32[]{:T(128)}, f32[]{:T(128)}) all-reduce(f32[]{:T(128)} %get-tuple-element.26, f32[]{:T(128)} %get-tuple-element.27), channel_id=1, replica_groups=mesh['px_0'=8,'px_1'=2,'py_0'=4,'py_1'=4] {'py_1'}, use_global_device_ids=true, to_apply=%region_46.47 | all-reduce | flops 2 | bytes 16 | tf_op jit(solution)/shard_map/psum | solution.py:54
  (515 shorter events, 371.7 us)
Async XLA Ops:
  1.5 19.3 %collective-permute-start.1 = (f32[2,8,1024]{2,1,0:T(8,128)S(1)}, f32[2,8,1024]{2,1,0:T(8,128)S(1)}, u32[]{:S(2)}, u32[]{:S(2)}) collective-permute-start(f32[2,8,1024]{2,1,0:T(8,128)S(1)} %get-tuple-element.165), channel_id=1, source_target_pairs={{16,0},{32,16},{48,32},{64,48},{80,64},{96,80},{112,96},{128,112},... | collective-permute-start | bytes 196616 | tf_op jit(solution)/shard_map/ppermute | solution.py:45
  2.8 17.1 %collective-permute-start = (f32[2,8,1024]{2,1,0:T(8,128)S(1)}, f32[2,8,1024]{2,1,0:T(8,128)S(1)}, u32[]{:S(2)}, u32[]{:S(2)}) collective-permute-start(f32[2,8,1024]{2,1,0:T(8,128)S(1)} %get-tuple-element.166), channel_id=1, source_target_pairs={{0,16},{16,32},{32,48},{48,64},{64,80},{80,96},{96,112},{112,128},... | collective-permute-start | bytes 196616 | tf_op jit(solution)/shard_map/ppermute | solution.py:43
  14.0 12.7 %collective-permute-start.6 = (f32[8,2,1024]{2,1,0:T(2,128)S(1)}, f32[8,2,1024]{2,1,0:T(2,128)S(1)}, u32[]{:S(2)}, u32[]{:S(2)}) collective-permute-start(f32[8,2,1024]{2,1,0:T(2,128)S(1)} %get-tuple-element.103), channel_id=1, source_target_pairs={{0,1},{1,2},{2,3},{3,4},{4,5},{5,6},{6,7},{7,8},{8,9},{9,10},{10,1... | collective-permute-start | bytes 196616 | tf_op jit(solution)/shard_map/ppermute | solution.py:43
  58.9 13.3 %collective-permute-start.14 = (f32[3,2,1,128]{3,2,1,0:T(1,128)S(1)}, f32[3,2,1,128]{3,2,1,0:T(1,128)S(1)}, u32[]{:S(2)}, u32[]{:S(2)}) collective-permute-start(f32[3,2,1,128]{3,2,1,0:T(1,128)S(1)} %get-tuple-element.193), channel_id=1, source_target_pairs={{1,0},{2,1},{3,2},{4,3},{5,4},{6,5},{7,6},{8,7},{9,8},{10,9},{11,1... | collective-permute-start | bytes 9224 | tf_op jit(solution)/shard_map/ppermute | solution.py:24
  60.8 11.3 %collective-permute-start.15 = (f32[3,2,1,128]{3,2,1,0:T(1,128)S(1)}, f32[3,2,1,128]{3,2,1,0:T(1,128)S(1)}, u32[]{:S(2)}, u32[]{:S(2)}) collective-permute-start(f32[3,2,1,128]{3,2,1,0:T(1,128)S(1)} %get-tuple-element.194), channel_id=1, source_target_pairs={{0,1},{1,2},{2,3},{3,4},{4,5},{5,6},{6,7},{7,8},{8,9},{9,10},{10,1... | collective-permute-start | bytes 9224 | tf_op jit(solution)/shard_map/ppermute | solution.py:23
  81.7 19.3 %collective-permute-start.17 = (f32[1,8,1024]{2,1,0:T(8,128)S(1)}, f32[1,8,1024]{2,1,0:T(8,128)S(1)}, u32[]{:S(2)}, u32[]{:S(2)}) collective-permute-start(f32[1,8,1024]{2,1,0:T(8,128)S(1)} %get-tuple-element.161), channel_id=1, source_target_pairs={{0,16},{16,32},{32,48},{48,64},{64,80},{80,96},{96,112},{112,128},... | collective-permute-start | bytes 98312 | tf_op jit(solution)/shard_map/ppermute | solution.py:23
  85.8 15.2 %collective-permute-start.16 = (f32[1,8,1024]{2,1,0:T(8,128)S(1)}, f32[1,8,1024]{2,1,0:T(8,128)S(1)}, u32[]{:S(2)}, u32[]{:S(2)}) collective-permute-start(f32[1,8,1024]{2,1,0:T(8,128)S(1)} %get-tuple-element.162), channel_id=1, source_target_pairs={{16,0},{32,16},{48,32},{64,48},{80,64},{96,80},{112,96},{128,112},... | collective-permute-start | bytes 98312 | tf_op jit(solution)/shard_map/ppermute | solution.py:24
  101.4 13.1 %collective-permute-start.21 = (f32[1,8,1024]{2,1,0:T(8,128)S(1)}, f32[1,8,1024]{2,1,0:T(8,128)S(1)}, u32[]{:S(2)}, u32[]{:S(2)}) collective-permute-start(f32[1,8,1024]{2,1,0:T(8,128)S(1)} %get-tuple-element.157), channel_id=1, source_target_pairs={{0,16},{16,32},{32,48},{48,64},{64,80},{80,96},{96,112},{112,128},... | collective-permute-start | bytes 98312 | tf_op jit(solution)/shard_map/ppermute | solution.py:23
  116.0 15.3 %collective-permute-start.25 = (f32[1,8,1024]{2,1,0:T(8,128)S(1)}, f32[1,8,1024]{2,1,0:T(8,128)S(1)}, u32[]{:S(2)}, u32[]{:S(2)}) collective-permute-start(f32[1,8,1024]{2,1,0:T(8,128)S(1)} %get-tuple-element.153), channel_id=1, source_target_pairs={{0,16},{16,32},{32,48},{48,64},{64,80},{80,96},{96,112},{112,128},... | collective-permute-start | bytes 98312 | tf_op jit(solution)/shard_map/ppermute | solution.py:23
  203.2 19.5 %collective-permute-start.41 = (f32[1,8,1024]{2,1,0:T(8,128)S(1)}, f32[1,8,1024]{2,1,0:T(8,128)S(1)}, u32[]{:S(2)}, u32[]{:S(2)}) collective-permute-start(f32[1,8,1024]{2,1,0:T(8,128)S(1)} %get-tuple-element.145), channel_id=1, source_target_pairs={{0,16},{16,32},{32,48},{48,64},{64,80},{80,96},{96,112},{112,128},... | collective-permute-start | bytes 98312 | tf_op jit(solution)/shard_map/ppermute | solution.py:23
  207.8 14.9 %collective-permute-start.40 = (f32[1,8,1024]{2,1,0:T(8,128)S(1)}, f32[1,8,1024]{2,1,0:T(8,128)S(1)}, u32[]{:S(2)}, u32[]{:S(2)}) collective-permute-start(f32[1,8,1024]{2,1,0:T(8,128)S(1)} %get-tuple-element.146), channel_id=1, source_target_pairs={{16,0},{32,16},{48,32},{64,48},{80,64},{96,80},{112,96},{128,112},... | collective-permute-start | bytes 98312 | tf_op jit(solution)/shard_map/ppermute | solution.py:24
  223.1 15.4 %collective-permute-start.45 = (f32[1,8,1024]{2,1,0:T(8,128)S(1)}, f32[1,8,1024]{2,1,0:T(8,128)S(1)}, u32[]{:S(2)}, u32[]{:S(2)}) collective-permute-start(f32[1,8,1024]{2,1,0:T(8,128)S(1)} %get-tuple-element.141), channel_id=1, source_target_pairs={{0,16},{16,32},{32,48},{48,64},{64,80},{80,96},{96,112},{112,128},... | collective-permute-start | bytes 98312 | tf_op jit(solution)/shard_map/ppermute | solution.py:23
  240.1 66.1 %collective-permute-start.49 = (f32[1,8,1024]{2,1,0:T(8,128)S(1)}, f32[1,8,1024]{2,1,0:T(8,128)S(1)}, u32[]{:S(2)}, u32[]{:S(2)}) collective-permute-start(f32[1,8,1024]{2,1,0:T(8,128)S(1)} %get-tuple-element.137), channel_id=1, source_target_pairs={{0,16},{16,32},{32,48},{48,64},{64,80},{80,96},{96,112},{112,128},... | collective-permute-start | bytes 98312 | tf_op jit(solution)/shard_map/ppermute | solution.py:23
  246.0 60.1 %collective-permute-start.48 = (f32[1,8,1024]{2,1,0:T(8,128)S(1)}, f32[1,8,1024]{2,1,0:T(8,128)S(1)}, u32[]{:S(2)}, u32[]{:S(2)}) collective-permute-start(f32[1,8,1024]{2,1,0:T(8,128)S(1)} %get-tuple-element.138), channel_id=1, source_target_pairs={{16,0},{32,16},{48,32},{64,48},{80,64},{96,80},{112,96},{128,112},... | collective-permute-start | bytes 98312 | tf_op jit(solution)/shard_map/ppermute | solution.py:24
  247.4 58.7 %collective-permute-start.51 = (f32[4,1,1024]{2,1,0:T(1,128)S(1)}, f32[4,1,1024]{2,1,0:T(1,128)S(1)}, u32[]{:S(2)}, u32[]{:S(2)}) collective-permute-start(f32[4,1,1024]{2,1,0:T(1,128)S(1)} %get-tuple-element.139), channel_id=1, source_target_pairs={{0,1},{1,2},{2,3},{3,4},{4,5},{5,6},{6,7},{7,8},{8,9},{9,10},{10,1... | collective-permute-start | bytes 49160 | tf_op jit(solution)/shard_map/ppermute | solution.py:23
  251.0 55.1 %collective-permute-start.50 = (f32[4,1,1024]{2,1,0:T(1,128)S(1)}, f32[4,1,1024]{2,1,0:T(1,128)S(1)}, u32[]{:S(2)}, u32[]{:S(2)}) collective-permute-start(f32[4,1,1024]{2,1,0:T(1,128)S(1)} %get-tuple-element.140), channel_id=1, source_target_pairs={{1,0},{2,1},{3,2},{4,3},{5,4},{6,5},{7,6},{8,7},{9,8},{10,9},{11,1... | collective-permute-start | bytes 49160 | tf_op jit(solution)/shard_map/ppermute | solution.py:24
  347.9 12.7 %collective-permute-start.62 = (f32[3,2,1,128]{3,2,1,0:T(1,128)S(1)}, f32[3,2,1,128]{3,2,1,0:T(1,128)S(1)}, u32[]{:S(2)}, u32[]{:S(2)}) collective-permute-start(f32[3,2,1,128]{3,2,1,0:T(1,128)S(1)} %get-tuple-element.177), channel_id=1, source_target_pairs={{1,0},{2,1},{3,2},{4,3},{5,4},{6,5},{7,6},{8,7},{9,8},{10,9},{11,1... | collective-permute-start | bytes 9224 | tf_op jit(solution)/shard_map/ppermute | solution.py:24
  371.3 19.3 %collective-permute-start.65 = (f32[1,8,1024]{2,1,0:T(8,128)S(1)}, f32[1,8,1024]{2,1,0:T(8,128)S(1)}, u32[]{:S(2)}, u32[]{:S(2)}) collective-permute-start(f32[1,8,1024]{2,1,0:T(8,128)S(1)} %get-tuple-element.129), channel_id=1, source_target_pairs={{0,16},{16,32},{32,48},{48,64},{64,80},{80,96},{96,112},{112,128},... | collective-permute-start | bytes 98312 | tf_op jit(solution)/shard_map/ppermute | solution.py:23
  375.4 15.2 %collective-permute-start.64 = (f32[1,8,1024]{2,1,0:T(8,128)S(1)}, f32[1,8,1024]{2,1,0:T(8,128)S(1)}, u32[]{:S(2)}, u32[]{:S(2)}) collective-permute-start(f32[1,8,1024]{2,1,0:T(8,128)S(1)} %get-tuple-element.130), channel_id=1, source_target_pairs={{16,0},{32,16},{48,32},{64,48},{80,64},{96,80},{112,96},{128,112},... | collective-permute-start | bytes 98312 | tf_op jit(solution)/shard_map/ppermute | solution.py:24
  391.1 13.1 %collective-permute-start.69 = (f32[1,8,1024]{2,1,0:T(8,128)S(1)}, f32[1,8,1024]{2,1,0:T(8,128)S(1)}, u32[]{:S(2)}, u32[]{:S(2)}) collective-permute-start(f32[1,8,1024]{2,1,0:T(8,128)S(1)} %get-tuple-element.125), channel_id=1, source_target_pairs={{0,16},{16,32},{32,48},{48,64},{64,80},{80,96},{96,112},{112,128},... | collective-permute-start | bytes 98312 | tf_op jit(solution)/shard_map/ppermute | solution.py:23
  405.7 64.3 %collective-permute-start.73 = (f32[1,8,1024]{2,1,0:T(8,128)S(1)}, f32[1,8,1024]{2,1,0:T(8,128)S(1)}, u32[]{:S(2)}, u32[]{:S(2)}) collective-permute-start(f32[1,8,1024]{2,1,0:T(8,128)S(1)} %get-tuple-element.121), channel_id=1, source_target_pairs={{0,16},{16,32},{32,48},{48,64},{64,80},{80,96},{96,112},{112,128},... | collective-permute-start | bytes 98312 | tf_op jit(solution)/shard_map/ppermute | solution.py:23
  409.3 60.6 %collective-permute-start.72 = (f32[1,8,1024]{2,1,0:T(8,128)S(1)}, f32[1,8,1024]{2,1,0:T(8,128)S(1)}, u32[]{:S(2)}, u32[]{:S(2)}) collective-permute-start(f32[1,8,1024]{2,1,0:T(8,128)S(1)} %get-tuple-element.122), channel_id=1, source_target_pairs={{16,0},{32,16},{48,32},{64,48},{80,64},{96,80},{112,96},{128,112},... | collective-permute-start | bytes 98312 | tf_op jit(solution)/shard_map/ppermute | solution.py:24
  410.7 59.2 %collective-permute-start.75 = (f32[4,1,1024]{2,1,0:T(1,128)S(1)}, f32[4,1,1024]{2,1,0:T(1,128)S(1)}, u32[]{:S(2)}, u32[]{:S(2)}) collective-permute-start(f32[4,1,1024]{2,1,0:T(1,128)S(1)} %get-tuple-element.123), channel_id=1, source_target_pairs={{0,1},{1,2},{2,3},{3,4},{4,5},{5,6},{6,7},{7,8},{8,9},{9,10},{10,1... | collective-permute-start | bytes 49160 | tf_op jit(solution)/shard_map/ppermute | solution.py:23
  414.3 55.6 %collective-permute-start.74 = (f32[4,1,1024]{2,1,0:T(1,128)S(1)}, f32[4,1,1024]{2,1,0:T(1,128)S(1)}, u32[]{:S(2)}, u32[]{:S(2)}) collective-permute-start(f32[4,1,1024]{2,1,0:T(1,128)S(1)} %get-tuple-element.124), channel_id=1, source_target_pairs={{1,0},{2,1},{3,2},{4,3},{5,4},{6,5},{7,6},{8,7},{9,8},{10,9},{11,1... | collective-permute-start | bytes 49160 | tf_op jit(solution)/shard_map/ppermute | solution.py:24
  507.1 13.3 %collective-permute-start.86 = (f32[3,2,1,128]{3,2,1,0:T(1,128)S(1)}, f32[3,2,1,128]{3,2,1,0:T(1,128)S(1)}, u32[]{:S(2)}, u32[]{:S(2)}) collective-permute-start(f32[3,2,1,128]{3,2,1,0:T(1,128)S(1)} %get-tuple-element.169), channel_id=1, source_target_pairs={{1,0},{2,1},{3,2},{4,3},{5,4},{6,5},{7,6},{8,7},{9,8},{10,9},{11,1... | collective-permute-start | bytes 9224 | tf_op jit(solution)/shard_map/ppermute | solution.py:24
  526.9 19.3 %collective-permute-start.89 = (f32[1,8,1024]{2,1,0:T(8,128)S(1)}, f32[1,8,1024]{2,1,0:T(8,128)S(1)}, u32[]{:S(2)}, u32[]{:S(2)}) collective-permute-start(f32[1,8,1024]{2,1,0:T(8,128)S(1)} %get-tuple-element.113), channel_id=1, source_target_pairs={{0,16},{16,32},{32,48},{48,64},{64,80},{80,96},{96,112},{112,128},... | collective-permute-start | bytes 98312 | tf_op jit(solution)/shard_map/ppermute | solution.py:23
  531.0 15.2 %collective-permute-start.88 = (f32[1,8,1024]{2,1,0:T(8,128)S(1)}, f32[1,8,1024]{2,1,0:T(8,128)S(1)}, u32[]{:S(2)}, u32[]{:S(2)}) collective-permute-start(f32[1,8,1024]{2,1,0:T(8,128)S(1)} %get-tuple-element.114), channel_id=1, source_target_pairs={{16,0},{32,16},{48,32},{64,48},{80,64},{96,80},{112,96},{128,112},... | collective-permute-start | bytes 98312 | tf_op jit(solution)/shard_map/ppermute | solution.py:24
  546.7 13.1 %collective-permute-start.93 = (f32[1,8,1024]{2,1,0:T(8,128)S(1)}, f32[1,8,1024]{2,1,0:T(8,128)S(1)}, u32[]{:S(2)}, u32[]{:S(2)}) collective-permute-start(f32[1,8,1024]{2,1,0:T(8,128)S(1)} %get-tuple-element.109), channel_id=1, source_target_pairs={{0,16},{16,32},{32,48},{48,64},{64,80},{80,96},{96,112},{112,128},... | collective-permute-start | bytes 98312 | tf_op jit(solution)/shard_map/ppermute | solution.py:23
  561.2 63.8 %collective-permute-start.97 = (f32[1,8,1024]{2,1,0:T(8,128)S(1)}, f32[1,8,1024]{2,1,0:T(8,128)S(1)}, u32[]{:S(2)}, u32[]{:S(2)}) collective-permute-start(f32[1,8,1024]{2,1,0:T(8,128)S(1)} %get-tuple-element.105), channel_id=1, source_target_pairs={{0,16},{16,32},{32,48},{48,64},{64,80},{80,96},{96,112},{112,128},... | collective-permute-start | bytes 98312 | tf_op jit(solution)/shard_map/ppermute | solution.py:23
  564.9 60.1 %collective-permute-start.96 = (f32[1,8,1024]{2,1,0:T(8,128)S(1)}, f32[1,8,1024]{2,1,0:T(8,128)S(1)}, u32[]{:S(2)}, u32[]{:S(2)}) collective-permute-start(f32[1,8,1024]{2,1,0:T(8,128)S(1)} %get-tuple-element.106), channel_id=1, source_target_pairs={{16,0},{32,16},{48,32},{64,48},{80,64},{96,80},{112,96},{128,112},... | collective-permute-start | bytes 98312 | tf_op jit(solution)/shard_map/ppermute | solution.py:24
  566.2 58.7 %collective-permute-start.99 = (f32[4,1,1024]{2,1,0:T(1,128)S(1)}, f32[4,1,1024]{2,1,0:T(1,128)S(1)}, u32[]{:S(2)}, u32[]{:S(2)}) collective-permute-start(f32[4,1,1024]{2,1,0:T(1,128)S(1)} %get-tuple-element.107), channel_id=1, source_target_pairs={{0,1},{1,2},{2,3},{3,4},{4,5},{5,6},{6,7},{7,8},{8,9},{9,10},{10,1... | collective-permute-start | bytes 49160 | tf_op jit(solution)/shard_map/ppermute | solution.py:23
  569.9 55.1 %collective-permute-start.98 = (f32[4,1,1024]{2,1,0:T(1,128)S(1)}, f32[4,1,1024]{2,1,0:T(1,128)S(1)}, u32[]{:S(2)}, u32[]{:S(2)}) collective-permute-start(f32[4,1,1024]{2,1,0:T(1,128)S(1)} %get-tuple-element.108), channel_id=1, source_target_pairs={{1,0},{2,1},{3,2},{4,3},{5,4},{6,5},{7,6},{8,7},{9,8},{10,9},{11,1... | collective-permute-start | bytes 49160 | tf_op jit(solution)/shard_map/ppermute | solution.py:24
  (119 other events, 3481.5 us)
where the time goes:
time: 684 us; the launch traced here: 672 us
  starting transfers between devices  281 us (41%)
  blocking collectives  190 us (28%)
  waiting for transfers between devices  93.3 us (14%)
  local copies, waits for them, and re-layouts  55.5 us (8%)
  other arithmetic  34.7 us (5%)
  between operations  17.3 us (3%)
    psum x16, blocking collectives, by_axis(): value = lax.psum(value, axis)  190 us
    ppermute x40, starting transfers between devices, padded_2(): lax.ppermute(last, axis, up)  157 us
    ppermute x40, starting transfers between devices, padded_2(): lax.ppermute(first, axis, [(b, a) for a, b in up])  73.7 us
    ppermute x40, waiting for transfers between devices, padded_2(): lax.ppermute(first, axis, [(b, a) for a, b in up])  66.1 us
    ppermute x10, starting transfers between devices, with_halo(): lax.ppermute(tail, axis, [(i, (i + 1) % count) for i in range(ends)])  28.7 us
    ppermute x10, waiting for transfers between devices, with_halo(): lax.ppermute(head, axis, [((i + 1) % count, i) for i in range(ends)])  25.5 us
    reshape x12, local copies, waits for them, and re-layouts, box_sum(): values.reshape(rows_agg, 2, cols_agg, 4, depth_agg, 8).sum(axis=(1, 3, 5))  22.2 us
    ppermute x10, starting transfers between devices, with_halo(): lax.ppermute(head, axis, [((i + 1) % count, i) for i in range(ends)])  21.8 us
  transfers between devices with their start and end apart: 100, of which 29 were waited for; matrix products, arithmetic and copies ran while one was open for 1% of the time, Pallas kernels for 0%

commit v1 on v0

--- a/solution.py
+++ b/solution.py
@@ -10,6 +10,12 @@
 PY = ("py_0", "py_1")
 OMEGA = 2.0 / 3.0
 FACES = (32.0, 16.0, 8.0)
+
+
+def summed_here(x, mesh_axis):
+    blocks = lax.all_gather(x, mesh_axis, axis=0, tiled=False)
+    total = blocks.sum(axis=0)
+    return total
 
 
 def padded_2(value, sides, width):
@@ -51,7 +57,7 @@
 
 def by_axis(value, axes):
     for axis in axes:
-        value = lax.psum(value, axis)
+        value = summed_here(value, axis)
     return value
 
 

time: 684 us -> 737 us (1.077)
  local copies, waits for them, and re-layouts: 55.5 us -> 106 us
  waiting for transfers between devices: 93.3 us -> 43.4 us
  starting transfers between devices: 281 us -> 316 us
  other arithmetic: 34.7 us -> 56.5 us
    psum x16 -> x0, blocking collectives: 190 us -> none  [by_axis(): value = lax.psum(value, axis)]
    unnamed x0 -> x16, blocking collectives: none -> 184 us
    ppermute x40, waiting for transfers between devices: 66.1 us -> 0.11 us  [padded_2(): lax.ppermute(first, axis, [(b, a) for a, b in up])]
    unnamed x106 -> x188, local copies, waits for them, and re-layouts: 3.48 us -> 49.6 us
    ppermute x40, starting transfers between devices: 157 us -> 195 us  [padded_2(): lax.ppermute(last, axis, up)]
    reduce_sum x0 -> x32, other arithmetic: none -> 20.1 us  [summed_here(): total = blocks.sum(axis=0)]
    ppermute x40, waiting for transfers between devices: 0.11 us -> 18.6 us  [padded_2(): lax.ppermute(last, axis, up)]
  transfers between devices with their start and end apart: 100 -> 100, of which waited for: 29 -> 27; matrix products, arithmetic and copies ran while one was open for 1% -> 7% of each run, Pallas kernels for 0% -> 0%
where the time goes in v1:
time: 737 us; the launch traced here: 724 us
  starting transfers between devices  316 us (43%)
  blocking collectives  184 us (25%)
  local copies, waits for them, and re-layouts  106 us (14%)
  other arithmetic  56.5 us (8%)
  waiting for transfers between devices  43.4 us (6%)
  between operations  17.6 us (2%)
    ppermute x40, starting transfers between devices, padded_2(): lax.ppermute(last, axis, up)  195 us
    unnamed x16, blocking collectives  184 us
    ppermute x40, starting transfers between devices, padded_2(): lax.ppermute(first, axis, [(b, a) for a, b in up])  71.9 us
    unnamed x188, local copies, waits for them, and re-layouts  49.6 us
    ppermute x10, starting transfers between devices, with_halo(): lax.ppermute(tail, axis, [(i, (i + 1) % count) for i in range(ends)])  28.9 us
    reshape x12, local copies, waits for them, and re-layouts, box_sum(): values.reshape(rows_agg, 2, cols_agg, 4, depth_agg, 8).sum(axis=(1, 3, 5))  26.2 us
    ppermute x10, waiting for transfers between devices, with_halo(): lax.ppermute(head, axis, [((i + 1) % count, i) for i in range(ends)])  23.8 us
    ppermute x10, starting transfers between devices, with_halo(): lax.ppermute(head, axis, [((i + 1) % count, i) for i in range(ends)])  21.1 us
  transfers between devices with their start and end apart: 100, of which 27 were waited for; matrix products, arithmetic and copies ran while one was open for 7% of the time, Pallas kernels for 0%

profile of v1, /device:TPU:8, one launch (start us, length us, event | category | flops | bytes accessed | tf_op | source)
XLA Modules:
  0.0 723.6 jit_solution(8175337163140676275)
XLA Ops:
  54.7 6.1 collective-permute-start.15
  62.1 5.6 collective-permute-start.13
  85.1 6.0 collective-permute-start.19
  100.3 6.0 collective-permute-start.23
  115.9 5.8 collective-permute-start.27
  131.1 6.2 collective-permute-start.30
  139.3 6.4 collective-permute-done.31
  159.8 6.3 collective-permute-start.35
  174.3 5.8 collective-permute-start.39
  181.3 7.0 collective-permute-start.37
  205.2 6.0 collective-permute-start.43
  220.7 5.8 collective-permute-start.47
  230.8 5.3 collective-permute-start.49
  238.0 6.0 collective-permute-start.51
  248.0 25.1 %all-reduce.127 = (f32[8]{0:T(128)S(1)}, f32[8]{0:T(128)S(1)}) all-reduce(f32[8]{0:T(128)S(1)} %dynamic-update-slice, f32[8]{0:T(128)S(1)} %dynamic-update-slice.4), channel_id=1, replica_groups=mesh['px_0'=8,'px_1'=2,'py_0'=4,'py_1'=4] {'px_0'}, use_global_device_ids=true, to_apply=%add.92 | all-reduce | flops 16 | bytes 128
  284.6 15.3 %all-reduce.135 = (f32[4]{0:T(128)S(1)}, f32[4]{0:T(128)S(1)}) all-reduce(f32[4]{0:T(128)S(1)} %dynamic-update-slice.2, f32[4]{0:T(128)S(1)} %dynamic-update-slice.6), channel_id=1, replica_groups=mesh['px_0'=8,'px_1'=2,'py_0'=4,'py_1'=4] {'py_0'}, use_global_device_ids=true, to_apply=%add.94 | all-reduce | flops 8 | bytes 64
  303.8 9.7 %all-reduce.131 = (f32[4]{0:T(128)S(1)}, f32[4]{0:T(128)S(1)}) all-reduce(f32[4]{0:T(128)S(1)} %dynamic-update-slice.3, f32[4]{0:T(128)S(1)} %dynamic-update-slice.7), channel_id=1, replica_groups=mesh['px_0'=8,'px_1'=2,'py_0'=4,'py_1'=4] {'py_1'}, use_global_device_ids=true, to_apply=%add.95 | all-reduce | flops 8 | bytes 64
  390.3 5.7 collective-permute-start.67
  405.3 6.0 collective-permute-start.71
  421.1 5.8 collective-permute-start.75
  430.0 21.0 %all-reduce.126 = (f32[8]{0:T(128)S(1)}, f32[8]{0:T(128)S(1)}) all-reduce(f32[8]{0:T(128)S(1)} %dynamic-update-slice.8, f32[8]{0:T(128)S(1)} %dynamic-update-slice.12), channel_id=1, replica_groups=mesh['px_0'=8,'px_1'=2,'py_0'=4,'py_1'=4] {'px_0'}, use_global_device_ids=true, to_apply=%add.100 | all-reduce | flops 16 | bytes 128
  461.1 13.9 %all-reduce.134 = (f32[4]{0:T(128)S(1)}, f32[4]{0:T(128)S(1)}) all-reduce(f32[4]{0:T(128)S(1)} %dynamic-update-slice.10, f32[4]{0:T(128)S(1)} %dynamic-update-slice.14), channel_id=1, replica_groups=mesh['px_0'=8,'px_1'=2,'py_0'=4,'py_1'=4] {'py_0'}, use_global_device_ids=true, to_apply=%add.102 | all-reduce | flops 8 | bytes 64
  478.7 9.7 %all-reduce.130 = (f32[4]{0:T(128)S(1)}, f32[4]{0:T(128)S(1)}) all-reduce(f32[4]{0:T(128)S(1)} %dynamic-update-slice.11, f32[4]{0:T(128)S(1)} %dynamic-update-slice.15), channel_id=1, replica_groups=mesh['px_0'=8,'px_1'=2,'py_0'=4,'py_1'=4] {'py_1'}, use_global_device_ids=true, to_apply=%add.103 | all-reduce | flops 8 | bytes 64
  559.5 6.0 collective-permute-start.91
  575.1 6.0 collective-permute-start.95
  590.7 5.8 collective-permute-start.99
  599.3 21.0 %all-reduce.125 = (f32[8]{0:T(128)S(1)}, f32[8]{0:T(128)S(1)}) all-reduce(f32[8]{0:T(128)S(1)} %dynamic-update-slice.16, f32[8]{0:T(128)S(1)} %dynamic-update-slice.20), channel_id=1, replica_groups=mesh['px_0'=8,'px_1'=2,'py_0'=4,'py_1'=4] {'px_0'}, use_global_device_ids=true, to_apply=%add.108 | all-reduce | flops 16 | bytes 128
  631.1 13.9 %all-reduce.133 = (f32[4]{0:T(128)S(1)}, f32[4]{0:T(128)S(1)}) all-reduce(f32[4]{0:T(128)S(1)} %dynamic-update-slice.18, f32[4]{0:T(128)S(1)} %dynamic-update-slice.22), channel_id=1, replica_groups=mesh['px_0'=8,'px_1'=2,'py_0'=4,'py_1'=4] {'py_0'}, use_global_device_ids=true, to_apply=%add.110 | all-reduce | flops 8 | bytes 64
  649.1 9.7 %all-reduce.129 = (f32[4]{0:T(128)S(1)}, f32[4]{0:T(128)S(1)}) all-reduce(f32[4]{0:T(128)S(1)} %dynamic-update-slice.19, f32[4]{0:T(128)S(1)} %dynamic-update-slice.23), channel_id=1, replica_groups=mesh['px_0'=8,'px_1'=2,'py_0'=4,'py_1'=4] {'py_1'}, use_global_device_ids=true, to_apply=%add.111 | all-reduce | flops 8 | bytes 64
  668.1 17.0 %all-reduce.124 = (f32[8]{0:T(128)S(1)}, f32[8]{0:T(128)S(1)}) all-reduce(f32[8]{0:T(128)S(1)} %dynamic-update-slice.24, f32[8]{0:T(128)S(1)} %dynamic-update-slice.28), channel_id=1, replica_groups=mesh['px_0'=8,'px_1'=2,'py_0'=4,'py_1'=4] {'px_0'}, use_global_device_ids=true, to_apply=%add.116 | all-reduce | flops 16 | bytes 128
  695.4 7.7 %all-reduce.132 = (f32[4]{0:T(128)S(1)}, f32[4]{0:T(128)S(1)}) all-reduce(f32[4]{0:T(128)S(1)} %dynamic-update-slice.26, f32[4]{0:T(128)S(1)} %dynamic-update-slice.30), channel_id=1, replica_groups=mesh['px_0'=8,'px_1'=2,'py_0'=4,'py_1'=4] {'py_0'}, use_global_device_ids=true, to_apply=%add.118 | all-reduce | flops 8 | bytes 64
  707.0 10.4 %all-reduce.128 = (f32[4]{0:T(128)S(1)}, f32[4]{0:T(128)S(1)}) all-reduce(f32[4]{0:T(128)S(1)} %dynamic-update-slice.27, f32[4]{0:T(128)S(1)} %dynamic-update-slice.31), channel_id=1, replica_groups=mesh['px_0'=8,'px_1'=2,'py_0'=4,'py_1'=4] {'py_1'}, use_global_device_ids=true, to_apply=%add.119 | all-reduce | flops 8 | bytes 64
  (629 shorter events, 412.0 us)
Async XLA Ops:
  52.7 15.1 %collective-permute-start.14 = (f32[3,2,1,128]{3,2,1,0:T(1,128)S(1)}, f32[3,2,1,128]{3,2,1,0:T(1,128)S(1)}, u32[]{:S(2)}, u32[]{:S(2)}) collective-permute-start(f32[3,2,1,128]{3,2,1,0:T(1,128)S(1)} %get-tuple-element.193), channel_id=1, source_target_pairs={{1,0},{2,1},{3,2},{4,3},{5,4},{6,5},{7,6},{8,7},{9,8},{10,9},{11,1... | collective-permute-start | bytes 9224 | tf_op jit(solution)/shard_map/ppermute | solution.py:30
  76.8 15.8 %collective-permute-start.16 = (f32[1,8,1024]{2,1,0:T(8,128)S(1)}, f32[1,8,1024]{2,1,0:T(8,128)S(1)}, u32[]{:S(2)}, u32[]{:S(2)}) collective-permute-start(f32[1,8,1024]{2,1,0:T(8,128)S(1)} %get-tuple-element.162), channel_id=1, source_target_pairs={{16,0},{32,16},{48,32},{64,48},{80,64},{96,80},{112,96},{128,112},... | collective-permute-start | bytes 98312 | tf_op jit(solution)/shard_map/ppermute | solution.py:30
  78.1 14.5 %collective-permute-start.17 = (f32[1,8,1024]{2,1,0:T(8,128)S(1)}, f32[1,8,1024]{2,1,0:T(8,128)S(1)}, u32[]{:S(2)}, u32[]{:S(2)}) collective-permute-start(f32[1,8,1024]{2,1,0:T(8,128)S(1)} %get-tuple-element.161), channel_id=1, source_target_pairs={{0,16},{16,32},{32,48},{48,64},{64,80},{80,96},{96,112},{112,128},... | collective-permute-start | bytes 98312 | tf_op jit(solution)/shard_map/ppermute | solution.py:29
  93.1 14.7 %collective-permute-start.20 = (f32[1,8,1024]{2,1,0:T(8,128)S(1)}, f32[1,8,1024]{2,1,0:T(8,128)S(1)}, u32[]{:S(2)}, u32[]{:S(2)}) collective-permute-start(f32[1,8,1024]{2,1,0:T(8,128)S(1)} %get-tuple-element.158), channel_id=1, source_target_pairs={{16,0},{32,16},{48,32},{64,48},{80,64},{96,80},{112,96},{128,112},... | collective-permute-start | bytes 98312 | tf_op jit(solution)/shard_map/ppermute | solution.py:30
  94.4 13.4 %collective-permute-start.21 = (f32[1,8,1024]{2,1,0:T(8,128)S(1)}, f32[1,8,1024]{2,1,0:T(8,128)S(1)}, u32[]{:S(2)}, u32[]{:S(2)}) collective-permute-start(f32[1,8,1024]{2,1,0:T(8,128)S(1)} %get-tuple-element.157), channel_id=1, source_target_pairs={{0,16},{16,32},{32,48},{48,64},{64,80},{80,96},{96,112},{112,128},... | collective-permute-start | bytes 98312 | tf_op jit(solution)/shard_map/ppermute | solution.py:29
  109.3 13.9 %collective-permute-start.24 = (f32[1,8,1024]{2,1,0:T(8,128)S(1)}, f32[1,8,1024]{2,1,0:T(8,128)S(1)}, u32[]{:S(2)}, u32[]{:S(2)}) collective-permute-start(f32[1,8,1024]{2,1,0:T(8,128)S(1)} %get-tuple-element.154), channel_id=1, source_target_pairs={{16,0},{32,16},{48,32},{64,48},{80,64},{96,80},{112,96},{128,112},... | collective-permute-start | bytes 98312 | tf_op jit(solution)/shard_map/ppermute | solution.py:30
  157.8 13.6 %collective-permute-start.34 = (f32[3,2,1,128]{3,2,1,0:T(1,128)S(1)}, f32[3,2,1,128]{3,2,1,0:T(1,128)S(1)}, u32[]{:S(2)}, u32[]{:S(2)}) collective-permute-start(f32[3,2,1,128]{3,2,1,0:T(1,128)S(1)} %get-tuple-element.189), channel_id=1, source_target_pairs={{1,0},{2,1},{3,2},{4,3},{5,4},{6,5},{7,6},{8,7},{9,8},{10,9},{11,1... | collective-permute-start | bytes 9224 | tf_op jit(solution)/shard_map/ppermute | solution.py:30
  172.3 16.0 %collective-permute-start.38 = (f32[3,2,1,128]{3,2,1,0:T(1,128)S(1)}, f32[3,2,1,128]{3,2,1,0:T(1,128)S(1)}, u32[]{:S(2)}, u32[]{:S(2)}) collective-permute-start(f32[3,2,1,128]{3,2,1,0:T(1,128)S(1)} %get-tuple-element.185), channel_id=1, source_target_pairs={{1,0},{2,1},{3,2},{4,3},{5,4},{6,5},{7,6},{8,7},{9,8},{10,9},{11,1... | collective-permute-start | bytes 9224 | tf_op jit(solution)/shard_map/ppermute | solution.py:30
  174.3 14.1 %collective-permute-start.39 = (f32[3,2,1,128]{3,2,1,0:T(1,128)S(1)}, f32[3,2,1,128]{3,2,1,0:T(1,128)S(1)}, u32[]{:S(2)}, u32[]{:S(2)}) collective-permute-start(f32[3,2,1,128]{3,2,1,0:T(1,128)S(1)} %get-tuple-element.186), channel_id=1, source_target_pairs={{0,1},{1,2},{2,3},{3,4},{4,5},{5,6},{6,7},{7,8},{8,9},{9,10},{10,1... | collective-permute-start | bytes 9224 | tf_op jit(solution)/shard_map/ppermute | solution.py:29
  197.0 15.8 %collective-permute-start.40 = (f32[1,8,1024]{2,1,0:T(8,128)S(1)}, f32[1,8,1024]{2,1,0:T(8,128)S(1)}, u32[]{:S(2)}, u32[]{:S(2)}) collective-permute-start(f32[1,8,1024]{2,1,0:T(8,128)S(1)} %get-tuple-element.146), channel_id=1, source_target_pairs={{16,0},{32,16},{48,32},{64,48},{80,64},{96,80},{112,96},{128,112},... | collective-permute-start | bytes 98312 | tf_op jit(solution)/shard_map/ppermute | solution.py:30
  198.3 14.5 %collective-permute-start.41 = (f32[1,8,1024]{2,1,0:T(8,128)S(1)}, f32[1,8,1024]{2,1,0:T(8,128)S(1)}, u32[]{:S(2)}, u32[]{:S(2)}) collective-permute-start(f32[1,8,1024]{2,1,0:T(8,128)S(1)} %get-tuple-element.145), channel_id=1, source_target_pairs={{0,16},{16,32},{32,48},{48,64},{64,80},{80,96},{96,112},{112,128},... | collective-permute-start | bytes 98312 | tf_op jit(solution)/shard_map/ppermute | solution.py:29
  213.2 14.7 %collective-permute-start.44 = (f32[1,8,1024]{2,1,0:T(8,128)S(1)}, f32[1,8,1024]{2,1,0:T(8,128)S(1)}, u32[]{:S(2)}, u32[]{:S(2)}) collective-permute-start(f32[1,8,1024]{2,1,0:T(8,128)S(1)} %get-tuple-element.142), channel_id=1, source_target_pairs={{16,0},{32,16},{48,32},{64,48},{80,64},{96,80},{112,96},{128,112},... | collective-permute-start | bytes 98312 | tf_op jit(solution)/shard_map/ppermute | solution.py:30
  214.5 13.4 %collective-permute-start.45 = (f32[1,8,1024]{2,1,0:T(8,128)S(1)}, f32[1,8,1024]{2,1,0:T(8,128)S(1)}, u32[]{:S(2)}, u32[]{:S(2)}) collective-permute-start(f32[1,8,1024]{2,1,0:T(8,128)S(1)} %get-tuple-element.141), channel_id=1, source_target_pairs={{0,16},{16,32},{32,48},{48,64},{64,80},{80,96},{96,112},{112,128},... | collective-permute-start | bytes 98312 | tf_op jit(solution)/shard_map/ppermute | solution.py:29
  229.5 86.7 %collective-permute-start.48 = (f32[1,8,1024]{2,1,0:T(8,128)S(1)}, f32[1,8,1024]{2,1,0:T(8,128)S(1)}, u32[]{:S(2)}, u32[]{:S(2)}) collective-permute-start(f32[1,8,1024]{2,1,0:T(8,128)S(1)} %get-tuple-element.138), channel_id=1, source_target_pairs={{16,0},{32,16},{48,32},{64,48},{80,64},{96,80},{112,96},{128,112},... | collective-permute-start | bytes 98312 | tf_op jit(solution)/shard_map/ppermute | solution.py:30
  230.8 85.4 %collective-permute-start.49 = (f32[1,8,1024]{2,1,0:T(8,128)S(1)}, f32[1,8,1024]{2,1,0:T(8,128)S(1)}, u32[]{:S(2)}, u32[]{:S(2)}) collective-permute-start(f32[1,8,1024]{2,1,0:T(8,128)S(1)} %get-tuple-element.137), channel_id=1, source_target_pairs={{0,16},{16,32},{32,48},{48,64},{64,80},{80,96},{96,112},{112,128},... | collective-permute-start | bytes 98312 | tf_op jit(solution)/shard_map/ppermute | solution.py:29
  236.1 80.0 %collective-permute-start.50 = (f32[4,1,1024]{2,1,0:T(1,128)S(1)}, f32[4,1,1024]{2,1,0:T(1,128)S(1)}, u32[]{:S(2)}, u32[]{:S(2)}) collective-permute-start(f32[4,1,1024]{2,1,0:T(1,128)S(1)} %get-tuple-element.140), channel_id=1, source_target_pairs={{1,0},{2,1},{3,2},{4,3},{5,4},{6,5},{7,6},{8,7},{9,8},{10,9},{11,1... | collective-permute-start | bytes 49160 | tf_op jit(solution)/shard_map/ppermute | solution.py:30
  238.0 78.1 %collective-permute-start.51 = (f32[4,1,1024]{2,1,0:T(1,128)S(1)}, f32[4,1,1024]{2,1,0:T(1,128)S(1)}, u32[]{:S(2)}, u32[]{:S(2)}) collective-permute-start(f32[4,1,1024]{2,1,0:T(1,128)S(1)} %get-tuple-element.139), channel_id=1, source_target_pairs={{0,1},{1,2},{2,3},{3,4},{4,5},{5,6},{6,7},{7,8},{8,9},{9,10},{10,1... | collective-permute-start | bytes 49160 | tf_op jit(solution)/shard_map/ppermute | solution.py:29
  381.7 15.8 %collective-permute-start.64 = (f32[1,8,1024]{2,1,0:T(8,128)S(1)}, f32[1,8,1024]{2,1,0:T(8,128)S(1)}, u32[]{:S(2)}, u32[]{:S(2)}) collective-permute-start(f32[1,8,1024]{2,1,0:T(8,128)S(1)} %get-tuple-element.130), channel_id=1, source_target_pairs={{16,0},{32,16},{48,32},{64,48},{80,64},{96,80},{112,96},{128,112},... | collective-permute-start | bytes 98312 | tf_op jit(solution)/shard_map/ppermute | solution.py:30
  383.0 14.5 %collective-permute-start.65 = (f32[1,8,1024]{2,1,0:T(8,128)S(1)}, f32[1,8,1024]{2,1,0:T(8,128)S(1)}, u32[]{:S(2)}, u32[]{:S(2)}) collective-permute-start(f32[1,8,1024]{2,1,0:T(8,128)S(1)} %get-tuple-element.129), channel_id=1, source_target_pairs={{0,16},{16,32},{32,48},{48,64},{64,80},{80,96},{96,112},{112,128},... | collective-permute-start | bytes 98312 | tf_op jit(solution)/shard_map/ppermute | solution.py:29
  398.0 14.8 %collective-permute-start.68 = (f32[1,8,1024]{2,1,0:T(8,128)S(1)}, f32[1,8,1024]{2,1,0:T(8,128)S(1)}, u32[]{:S(2)}, u32[]{:S(2)}) collective-permute-start(f32[1,8,1024]{2,1,0:T(8,128)S(1)} %get-tuple-element.126), channel_id=1, source_target_pairs={{16,0},{32,16},{48,32},{64,48},{80,64},{96,80},{112,96},{128,112},... | collective-permute-start | bytes 98312 | tf_op jit(solution)/shard_map/ppermute | solution.py:30
  414.3 79.9 %collective-permute-start.72 = (f32[1,8,1024]{2,1,0:T(8,128)S(1)}, f32[1,8,1024]{2,1,0:T(8,128)S(1)}, u32[]{:S(2)}, u32[]{:S(2)}) collective-permute-start(f32[1,8,1024]{2,1,0:T(8,128)S(1)} %get-tuple-element.122), channel_id=1, source_target_pairs={{16,0},{32,16},{48,32},{64,48},{80,64},{96,80},{112,96},{128,112},... | collective-permute-start | bytes 98312 | tf_op jit(solution)/shard_map/ppermute | solution.py:30
  415.7 78.5 %collective-permute-start.73 = (f32[1,8,1024]{2,1,0:T(8,128)S(1)}, f32[1,8,1024]{2,1,0:T(8,128)S(1)}, u32[]{:S(2)}, u32[]{:S(2)}) collective-permute-start(f32[1,8,1024]{2,1,0:T(8,128)S(1)} %get-tuple-element.121), channel_id=1, source_target_pairs={{0,16},{16,32},{32,48},{48,64},{64,80},{80,96},{96,112},{112,128},... | collective-permute-start | bytes 98312 | tf_op jit(solution)/shard_map/ppermute | solution.py:29
  419.2 75.0 %collective-permute-start.74 = (f32[4,1,1024]{2,1,0:T(1,128)S(1)}, f32[4,1,1024]{2,1,0:T(1,128)S(1)}, u32[]{:S(2)}, u32[]{:S(2)}) collective-permute-start(f32[4,1,1024]{2,1,0:T(1,128)S(1)} %get-tuple-element.124), channel_id=1, source_target_pairs={{1,0},{2,1},{3,2},{4,3},{5,4},{6,5},{7,6},{8,7},{9,8},{10,9},{11,1... | collective-permute-start | bytes 49160 | tf_op jit(solution)/shard_map/ppermute | solution.py:30
  421.1 73.1 %collective-permute-start.75 = (f32[4,1,1024]{2,1,0:T(1,128)S(1)}, f32[4,1,1024]{2,1,0:T(1,128)S(1)}, u32[]{:S(2)}, u32[]{:S(2)}) collective-permute-start(f32[4,1,1024]{2,1,0:T(1,128)S(1)} %get-tuple-element.123), channel_id=1, source_target_pairs={{0,1},{1,2},{2,3},{3,4},{4,5},{5,6},{6,7},{7,8},{8,9},{9,10},{10,1... | collective-permute-start | bytes 49160 | tf_op jit(solution)/shard_map/ppermute | solution.py:29
  551.2 15.8 %collective-permute-start.88 = (f32[1,8,1024]{2,1,0:T(8,128)S(1)}, f32[1,8,1024]{2,1,0:T(8,128)S(1)}, u32[]{:S(2)}, u32[]{:S(2)}) collective-permute-start(f32[1,8,1024]{2,1,0:T(8,128)S(1)} %get-tuple-element.114), channel_id=1, source_target_pairs={{16,0},{32,16},{48,32},{64,48},{80,64},{96,80},{112,96},{128,112},... | collective-permute-start | bytes 98312 | tf_op jit(solution)/shard_map/ppermute | solution.py:30
  552.5 14.5 %collective-permute-start.89 = (f32[1,8,1024]{2,1,0:T(8,128)S(1)}, f32[1,8,1024]{2,1,0:T(8,128)S(1)}, u32[]{:S(2)}, u32[]{:S(2)}) collective-permute-start(f32[1,8,1024]{2,1,0:T(8,128)S(1)} %get-tuple-element.113), channel_id=1, source_target_pairs={{0,16},{16,32},{32,48},{48,64},{64,80},{80,96},{96,112},{112,128},... | collective-permute-start | bytes 98312 | tf_op jit(solution)/shard_map/ppermute | solution.py:29
  567.5 15.0 %collective-permute-start.92 = (f32[1,8,1024]{2,1,0:T(8,128)S(1)}, f32[1,8,1024]{2,1,0:T(8,128)S(1)}, u32[]{:S(2)}, u32[]{:S(2)}) collective-permute-start(f32[1,8,1024]{2,1,0:T(8,128)S(1)} %get-tuple-element.110), channel_id=1, source_target_pairs={{16,0},{32,16},{48,32},{64,48},{80,64},{96,80},{112,96},{128,112},... | collective-permute-start | bytes 98312 | tf_op jit(solution)/shard_map/ppermute | solution.py:30
  569.0 13.6 %collective-permute-start.93 = (f32[1,8,1024]{2,1,0:T(8,128)S(1)}, f32[1,8,1024]{2,1,0:T(8,128)S(1)}, u32[]{:S(2)}, u32[]{:S(2)}) collective-permute-start(f32[1,8,1024]{2,1,0:T(8,128)S(1)} %get-tuple-element.109), channel_id=1, source_target_pairs={{0,16},{16,32},{32,48},{48,64},{64,80},{80,96},{96,112},{112,128},... | collective-permute-start | bytes 98312 | tf_op jit(solution)/shard_map/ppermute | solution.py:29
  584.1 80.0 %collective-permute-start.96 = (f32[1,8,1024]{2,1,0:T(8,128)S(1)}, f32[1,8,1024]{2,1,0:T(8,128)S(1)}, u32[]{:S(2)}, u32[]{:S(2)}) collective-permute-start(f32[1,8,1024]{2,1,0:T(8,128)S(1)} %get-tuple-element.106), channel_id=1, source_target_pairs={{16,0},{32,16},{48,32},{64,48},{80,64},{96,80},{112,96},{128,112},... | collective-permute-start | bytes 98312 | tf_op jit(solution)/shard_map/ppermute | solution.py:30
  585.4 78.7 %collective-permute-start.97 = (f32[1,8,1024]{2,1,0:T(8,128)S(1)}, f32[1,8,1024]{2,1,0:T(8,128)S(1)}, u32[]{:S(2)}, u32[]{:S(2)}) collective-permute-start(f32[1,8,1024]{2,1,0:T(8,128)S(1)} %get-tuple-element.105), channel_id=1, source_target_pairs={{0,16},{16,32},{32,48},{48,64},{64,80},{80,96},{96,112},{112,128},... | collective-permute-start | bytes 98312 | tf_op jit(solution)/shard_map/ppermute | solution.py:29
  588.8 75.1 %collective-permute-start.98 = (f32[4,1,1024]{2,1,0:T(1,128)S(1)}, f32[4,1,1024]{2,1,0:T(1,128)S(1)}, u32[]{:S(2)}, u32[]{:S(2)}) collective-permute-start(f32[4,1,1024]{2,1,0:T(1,128)S(1)} %get-tuple-element.108), channel_id=1, source_target_pairs={{1,0},{2,1},{3,2},{4,3},{5,4},{6,5},{7,6},{8,7},{9,8},{10,9},{11,1... | collective-permute-start | bytes 49160 | tf_op jit(solution)/shard_map/ppermute | solution.py:30
  590.7 73.3 %collective-permute-start.99 = (f32[4,1,1024]{2,1,0:T(1,128)S(1)}, f32[4,1,1024]{2,1,0:T(1,128)S(1)}, u32[]{:S(2)}, u32[]{:S(2)}) collective-permute-start(f32[4,1,1024]{2,1,0:T(1,128)S(1)} %get-tuple-element.107), channel_id=1, source_target_pairs={{0,1},{1,2},{2,3},{3,4},{4,5},{5,6},{6,7},{7,8},{8,9},{9,10},{10,1... | collective-permute-start | bytes 49160 | tf_op jit(solution)/shard_map/ppermute | solution.py:29
  (126 other events, 3766.6 us)
